TPU v7x, 32 devices: a whole 2x2x4 slice. The times are simulated.
32 devices in a mesh: groups: 2 (over x), ind: 16 (over z, y, core).
Axes of the slice: x: 2, y: 2, z: 4, core: 2. Of those that a mesh axis runs over, the one named last changes fastest.
Arguments:
- genotype: bfloat16 [12288, 16384], P(('groups', 'ind')), parts along dimension 0, may hold values from -4 to 4
- residual: bfloat16 [12288, 256], P(('groups', 'ind')), parts along dimension 0, may hold values from -4 to 4
- labels: int32 [12288, 256], P(('groups', 'ind')), parts along dimension 0, may hold values 0 or 1
- incl_old: float32 [32768, 256], P(('groups', 'ind')), parts along dimension 0, may hold values from 0.02 to 0.98
- mean_old: float32 [32768, 256], P(('groups', 'ind')), parts along dimension 0, may hold values from -0.078125 to 0.078125
- prior_logit: float32 [256], replicated, may hold values from -4 to 0
- slab_scale: float32 [256], replicated, may hold values from 0.25 to 8
- offset: float32 [256], replicated, may hold values from -2 to 1
Outputs:
- incl_new: float32 [32768, 256], P(('groups', 'ind')), parts along dimension 0
- mean_new: float32 [32768, 256], P(('groups', 'ind')), parts along dimension 0
- resid_new: float32 [12288, 256], P(('groups', 'ind')), parts along dimension 0
There are 2 independent parts, one for each index of `groups`. A program takes and returns all parts, laid end to end along the dimension named above; an argument that names none is the same for every part. Nothing has to cross between parts.
All inputs are finite; a program needn't handle non-finite values. No bound on the sum of `labels` on one device may be relied on, other than what follows from the above.
Results may differ from a plain program's by a relative error of at most 0.00062.
Values may be sent and summed in bfloat16 or wider, within the bound.
A program may use at most 128 MiB of HBM per device.

v0:
```python
import functools
import math

import jax
import jax.numpy as jnp
from jax import lax
from jax.experimental import pallas as pl
from jax.experimental.pallas import tpu as pltpu
from jax.sharding import PartitionSpec as P

LARGEST_TERM = 64.0


def sweep_kernel(
    n, chunks, wide_chunks,
    geno_hbm, resid_ref, incl_hbm, mean_hbm, prior_ref, scale_ref,
    stat_out, eta,
    geno, incl, mean, core_out, core_in, pair_out, pair_in, own, line_out, line_in, eff,
    geno_sem, in_sem, core_ss, core_rs, pair_ss, pair_rs, line_ss, line_rs,
    gz_ss, gz_rs, gy_ss, gy_rs, gc_ss, gc_rs,
):
    length = n // 4
    owned = incl.shape[0]
    rows = owned // chunks
    people = geno.shape[0]
    total = float(people * n)
    coding = 32760.0 / math.log(1.0 + LARGEST_TERM * total)
    me = lax.axis_index("ind")
    z = me // 4
    y = (me // 2) % 2
    c = me % 2

    def at(zz, yy, cc):
        return zz * 4 + yy * 2 + cc

    core_dev = {"ind": at(z, y, 1 - c)}
    pair_dev = {"ind": at(z, 1 - y, c)}
    up_dev = {"ind": at(lax.rem(z + 1, length), y, c)}
    down_dev = {"ind": at(lax.rem(z + length - 1, length), y, c)}
    has_up = z < length - 1
    has_down = z > 0

    def remote(src, dst, ss, rs, dev):
        return pltpu.make_async_remote_copy(
            src_ref=src, dst_ref=dst, send_sem=ss, recv_sem=rs,
            device_id=dev, device_id_type=pl.DeviceIdType.MESH,
        )

    def encode(x):
        code = (jnp.log(1.0 + jnp.abs(x)) * coding + 0.5).astype(jnp.int32)
        return jnp.where(x < 0.0, -code, code).astype(jnp.int16)

    def decode(code):
        level = code.astype(jnp.int32).astype(jnp.float32)
        size = jnp.exp(jnp.abs(level) * (1.0 / coding)) - 1.0
        return jnp.where(level < 0.0, -size, size)

    def cols(s, o):
        return pl.ds(pl.multiple_of(o * owned + s * rows, 128), rows)

    def load(s, o):
        return pltpu.make_async_copy(
            geno_hbm.at[:, cols(s, o)], geno.at[:, cols(s, o)], geno_sem.at[s, o]
        )

    def for_z(body):
        lax.fori_loop(0, length, lambda i, _: (body(i), 0)[1], 0)

    def loop(count, body):
        lax.fori_loop(0, count, lambda i, _: (body(i), 0)[1], 0)

    owners = ((1 - y, 1 - c), (y, 1 - c), (y, c), (1 - y, c))

    def load_chunk(s):
        for yy, cc in owners:
            for_z(lambda i: load(s, at(i, yy, cc)).start())

    loop(chunks, load_chunk)
    small = [
        pltpu.make_async_copy(incl_hbm, incl, in_sem.at[0]),
        pltpu.make_async_copy(mean_hbm, mean, in_sem.at[1]),
    ]
    for copy in small:
        copy.start()

    barrier = pltpu.get_barrier_semaphore()
    pl.semaphore_signal(barrier, inc=1, device_id=core_dev, device_id_type=pl.DeviceIdType.MESH)
    pl.semaphore_signal(barrier, inc=1, device_id=pair_dev, device_id_type=pl.DeviceIdType.MESH)

    @pl.when(has_up)
    def _():
        pl.semaphore_signal(barrier, inc=1, device_id=up_dev, device_id_type=pl.DeviceIdType.MESH)

    @pl.when(has_down)
    def _():
        pl.semaphore_signal(barrier, inc=1, device_id=down_dev, device_id_type=pl.DeviceIdType.MESH)

    pl.semaphore_wait(barrier, 2 + has_up.astype(jnp.int32) + has_down.astype(jnp.int32))

    def product(s, o):
        load(s, o).wait()
        return lax.dot_general(
            geno[:, cols(s, o)], resid_ref[...], (((0,), (0,)), ((), ())),
            preferred_element_type=jnp.float32,
        )

    def wide(s):
        return s >= chunks - wide_chunks

    def side(f):
        return jnp.where(f == 0, y, 1 - y)

    def core_copy(s, h):
        return remote(
            core_out.at[s % 2, h], core_in.at[s, h], core_ss.at[s, h], core_rs.at[s, h], core_dev
        )

    def pair_copy(s):
        return remote(pair_out.at[s], pair_in.at[s], pair_ss.at[s], pair_rs.at[s], pair_dev)

    def line_copy(s, t, d):
        return remote(
            line_out.at[s, t, d], line_in.at[s, t, d], line_ss.at[s, t, d], line_rs.at[s, t, d],
            up_dev if d == 0 else down_dev,
        )

    def first(s):
        def to_core(h):
            yy, cc = owners[h]

            @pl.when(s >= 2)
            def _():
                core_copy(s - 2, h).wait_send()

            def part(i):
                core_out[s % 2, h, i] = product(s, at(i, yy, cc))

            for_z(part)
            core_copy(s, h).start()

        to_core(0)

        def keep(i):
            own[s, i] = product(s, at(i, y, c))

        for_z(keep)
        core_copy(s, 0).wait_recv()

        def pass_on(i):
            pair_out[s, i] = encode(product(s, at(i, 1 - y, c)) + core_in[s, 0, i])

        for_z(pass_on)
        pair_copy(s).start()
        to_core(1)

    loop(chunks, first)
    for copy in small:
        copy.wait()
    eta[...] = jnp.zeros_like(eta)

    scale = scale_ref[...]
    shrink = scale / (1.0 + scale)
    bias = prior_ref[...] - 0.5 * jnp.log1p(scale)
    curve = 0.5 * total * shrink

    def along(s, t):
        @pl.when(t == 0)
        def _():
            core_copy(s, 1).wait_recv()
            pair_copy(s).wait_recv()

            def add(i):
                own[s, i] = own[s, i] + core_in[s, 1, i] + decode(pair_in[s, i])

            for_z(add)

        for d in range(2):
            place = z if d == 0 else length - 1 - z
            block = length - 1 - t + z if d == 0 else t - (length - 1 - z)

            @pl.when((place <= t) & (place < length - 1))
            def _():
                @pl.when(place == 0)
                def _():
                    line_out[s, t, d] = encode(own[s, block])

                @pl.when(place > 0)
                def _():
                    line_copy(s, t - 1, d).wait_recv()
                    line_out[s, t, d] = encode(own[s, block] + decode(line_in[s, t - 1, d]))

                line_copy(s, t, d).start()

    def gz_copy(s, u, d, f):
        k, o = 2 * s + f, at(z - u if d == 0 else z + u, side(f), c)
        return remote(
            eff.at[s, o], eff.at[s, o], gz_ss.at[k, u, d], gz_rs.at[k, u, d], up_dev if d == 0 else down_dev
        )

    def gz_landed(s, u, d, f):
        k, o = 2 * s + f, at(z - 1 - u if d == 0 else z + 1 + u, side(f), c)
        return remote(
            eff.at[s, o], eff.at[s, o], gz_ss.at[k, u, d], gz_rs.at[k, u, d], up_dev if d == 0 else down_dev
        )

    def gy_copy(s, i, yy):
        o = at(i, yy, c)
        return remote(eff.at[s, o], eff.at[s, o], gy_ss.at[s, i], gy_rs.at[s, i], pair_dev)

    def gc_copy(s, i, yy, cc):
        o = at(i, yy, cc)
        return remote(eff.at[s, o], eff.at[s, o], gc_ss.at[s, yy, i], gc_rs.at[s, yy, i], core_dev)

    def use(s, o):
        eta[...] += jnp.dot(geno[:, cols(s, o)], eff[s, o], preferred_element_type=jnp.float32)

    def send_own(s, f):
        @pl.when(has_up)
        def _():
            gz_copy(s, 0, 0, f).start()

        @pl.when(has_down)
        def _():
            gz_copy(s, 0, 1, f).start()

        gc_copy(s, z, side(f), c).start()

    def finish(s):
        for d in range(2):
            @pl.when(has_down if d == 0 else has_up)
            def _():
                line_copy(s, length - 2, d).wait_recv()
                own[s, z] = own[s, z] + decode(line_in[s, length - 2, d])

        here = pl.ds(pl.multiple_of(s * rows, 8), rows)
        before = incl[here, :]
        stat = own[s, z] / total + before * mean[here, :]
        stat_out[here, :] = stat
        incl_new = 0.5 * before + 0.5 * jax.nn.sigmoid(bias + curve * stat * stat)
        eff[s, me] = (incl_new * (stat * shrink)).astype(jnp.bfloat16)
        gy_copy(s, z, y).start()
        send_own(s, 0)
        use(s, me)

    def send_other(s):
        gy_copy(s, z, 1 - y).wait_recv()
        send_own(s, 1)
        use(s, at(z, 1 - y, c))

    def spread(s, u, f):
        for d in range(2):
            source = z - u if d == 0 else z + u

            @pl.when((source >= 0) & (source < length))
            def _():
                gz_landed(s, u - 1, d, f).wait_recv()

                @pl.when(has_up if d == 0 else has_down)
                def _():
                    gz_copy(s, u, d, f).start()

                @pl.when(jnp.logical_not(wide(s)))
                def _():
                    gy_copy(s, source, y).start()

                gc_copy(s, source, side(f), c).start()
                use(s, at(source, side(f), c))

    def within(s):
        return (s >= 0) & (s < chunks)

    def from_core(s):
        def take(i):
            for yy in range(2):
                gc_copy(s, i, yy, 1 - c).wait_recv()
                use(s, at(i, yy, 1 - c))

        for_z(take)

    def last(s):
        def take(i):
            gy_copy(s, i, 1 - y).wait_recv()
            gc_copy(s, i, 1 - y, c).start()
            use(s, at(i, 1 - y, c))

        @pl.when(jnp.logical_not(wide(s)))
        def _():
            for_z(take)

        @pl.when(s > 0)
        def _():
            from_core(s - 1)

    def wave(w):
        def gather_step(k):
            u = length - 1 - k
            s = w - (length - 1) - u

            @pl.when(within(s - 1) & wide(s - 1))
            def _():
                spread(s - 1, u, 1)

            @pl.when(within(s))
            def _():
                spread(s, u, 0)

        loop(length - 1, gather_step)
        here = w - (length - 1)

        @pl.when(within(here - 1) & wide(here - 1))
        def _():
            send_other(here - 1)

        @pl.when(within(here))
        def _():
            finish(here)

        def reduce_step(k):
            t = length - 2 - k

            @pl.when(within(w - t))
            def _():
                along(w - t, t)

        loop(length - 1, reduce_step)

        @pl.when(within(w - 2 * length + 1))
        def _():
            last(w - 2 * length + 1)

    loop(chunks + 2 * length - 1, wave)
    from_core(chunks - 1)

    def drain(s):
        @pl.when(s >= chunks - 2)
        def _():
            for h in range(2):
                core_copy(s, h).wait_send()

        pair_copy(s).wait_send()
        gy_copy(s, z, y).wait_send()

        @pl.when(jnp.logical_not(wide(s)))
        def _():
            def sent(i):
                @pl.when(i != z)
                def _():
                    gy_copy(s, i, y).wait_send()

            for_z(sent)

        def step(t):
            for d in range(2):
                place = z if d == 0 else length - 1 - z
                origin = z - t if d == 0 else z + t

                @pl.when((place <= t) & (place < length - 1))
                def _():
                    line_copy(s, t, d).wait_send()

                @pl.when((origin >= 0) & (origin < length) & (place < length - 1))
                def _():
                    gz_copy(s, t, d, 0).wait_send()

                    @pl.when(wide(s))
                    def _():
                        gz_copy(s, t, d, 1).wait_send()

        loop(length - 1, step)

        def blocks(i):
            for yy in range(2):
                gc_copy(s, i, yy, c).wait_send()

        for_z(blocks)

    loop(chunks, drain)


def outputs_kernel(
    half_total, stat_ref, incl_ref, eta_ref, labels_ref, prior_ref, scale_ref, offset_ref,
    incl_out, mean_out, resid_out,
):
    scale = scale_ref[...]
    shrink = scale / (1.0 + scale)
    bias = prior_ref[...] - 0.5 * jnp.log1p(scale)
    stat = stat_ref[...]
    mean_out[...] = stat * shrink
    logit = bias + (half_total * shrink) * stat * stat
    incl_out[...] = 0.5 * incl_ref[...] + 0.5 * jax.nn.sigmoid(logit)
    resid_out[...] = 4.0 * (
        labels_ref[...].astype(jnp.float32) - jax.nn.sigmoid(eta_ref[...] + offset_ref[...])
    )


def on_device(genotype, residual, labels, incl_old, mean_old, prior_logit, slab_scale, offset):
    n = lax.axis_size("ind")
    people, _ = genotype.shape
    owned, columns = incl_old.shape
    length = n // 4
    chunks = max(1, min(4, owned // 256))
    wide_chunks = 0
    rows = owned // chunks
    f32, bf16, i16 = jnp.float32, jnp.bfloat16, jnp.int16
    anywhere = pl.BlockSpec(memory_space=pl.ANY)
    vmem = pl.BlockSpec(memory_space=pltpu.VMEM)
    dma = pltpu.SemaphoreType.DMA
    hops = length - 1
    prior, scale, shift = (v.reshape(1, -1) for v in (prior_logit, slab_scale, offset))
    stat, eta = pl.pallas_call(
        functools.partial(sweep_kernel, n, chunks, wide_chunks),
        out_shape=(
            jax.ShapeDtypeStruct((owned, columns), f32),
            jax.ShapeDtypeStruct((people, columns), f32),
        ),
        in_specs=[anywhere, vmem, anywhere, anywhere, vmem, vmem],
        out_specs=(vmem, vmem),
        scratch_shapes=[
            pltpu.VMEM(genotype.shape, bf16),
            pltpu.VMEM(incl_old.shape, f32),
            pltpu.VMEM(mean_old.shape, f32),
            pltpu.VMEM((min(chunks, 2), 2, length, rows, columns), f32),
            pltpu.VMEM((chunks, 2, length, rows, columns), f32),
            pltpu.VMEM((chunks, length, rows, columns), i16),
            pltpu.VMEM((chunks, length, rows, columns), i16),
            pltpu.VMEM((chunks, length, rows, columns), f32),
            pltpu.VMEM((chunks, hops, 2, rows, columns), i16),
            pltpu.VMEM((chunks, hops, 2, rows, columns), i16),
            pltpu.VMEM((chunks, n, rows, columns), bf16),
            dma((chunks, n)),
            dma((2,)),
            dma((chunks, 2)),
            dma((chunks, 2)),
            dma((chunks,)),
            dma((chunks,)),
            dma((chunks, hops, 2)),
            dma((chunks, hops, 2)),
            dma((2 * chunks, hops, 2)),
            dma((2 * chunks, hops, 2)),
            dma((chunks, length)),
            dma((chunks, length)),
            dma((chunks, 2, length)),
            dma((chunks, 2, length)),
        ],
        compiler_params=pltpu.CompilerParams(
            collective_id=0, has_side_effects=True, vmem_limit_bytes=67043328
        ),
        name="sweep",
    )(genotype, residual, incl_old, mean_old, prior, scale)

    steps = 4 if owned % 32 == 0 and people % 32 == 0 else 1
    upper = pl.BlockSpec((owned // steps, columns), lambda i: (i, 0))
    lower = pl.BlockSpec((people // steps, columns), lambda i: (i, 0))
    flat = pl.BlockSpec((1, columns), lambda i: (0, 0))
    return pl.pallas_call(
        functools.partial(outputs_kernel, 0.5 * people * n),
        grid=(steps,),
        out_shape=(
            jax.ShapeDtypeStruct((owned, columns), f32),
            jax.ShapeDtypeStruct((owned, columns), f32),
            jax.ShapeDtypeStruct((people, columns), f32),
        ),
        in_specs=[upper, upper, lower, lower, flat, flat, flat],
        out_specs=(upper, upper, lower),
        name="outputs",
    )(stat, incl_old, eta, labels, prior, scale, shift)


def solution(mesh):
    placed = (
        P(("groups", "ind"), None),
        P(("groups", "ind"), None),
        P(("groups", "ind"), None),
        P(("groups", "ind"), None),
        P(("groups", "ind"), None),
        P(),
        P(),
        P(),
    )
    return jax.shard_map(
        on_device,
        mesh=mesh,
        in_specs=placed,
        out_specs=(
            P(("groups", "ind"), None),
            P(("groups", "ind"), None),
            P(("groups", "ind"), None),
        ),
        check_vma=False,
    )
```

profile of v0, /device:TPU:0, one launch (start us, length us, event | category | flops | bytes accessed | tf_op | source)
XLA Modules:
  0.0 115.0 jit_solution(4654424786767720904)
XLA Ops:
  0.6 110.4 %sweep.1 = (f32[1024,256]{1,0:T(8,128)}, f32[384,256]{1,0:T(8,128)}) custom-call(bf16[384,16384]{1,0:T(8,128)(2,1)} %geno_hbm.1, bf16[384,256]{1,0:T(8,128)(2,1)} %resid_ref.1, f32[1024,256]{1,0:T(8,128)} %incl_ref.1, f32[1024,256]{1,0:T(8,128)} %mean_hbm.1, f32[1,256]{1,0:T(1,128)} %bitcast.3, f32[1,256]{1,0:T(1,128)} %bitcast.5), custom_call_target="tpu_custom_call" | custom-call | tf_op jit(solution)/shard_map/sweep/pallas_call | solution.py:410
  111.1 4.0 %outputs.1 = (f32[1024,256]{1,0:T(8,128)}, f32[1024,256]{1,0:T(8,128)}, f32[384,256]{1,0:T(8,128)}) custom-call(f32[1024,256]{1,0:T(8,128)} %get-tuple-element.5.stat_ref, f32[1024,256]{1,0:T(8,128)} %incl_ref.1, f32[384,256]{1,0:T(8,128)} %get-tuple-element.6.eta_ref, s32[384,256]{1,0:T(8,128)} %labels_ref.1, f32[1,256]{1,0:T(1,128)} %bitcast.4, ...), custom_call_target="tpu_custom_call" | custom-call | tf_op jit(solution)/shard_map/outputs/pallas_call | solution.py:455
where the time goes:
time: 115 us
  Pallas kernels  114 us (99%)
    pallas_call x1, Pallas kernels, on_device(): pl.pallas_call(functools.partial(sweep_kernel, n, chunks, wide_chunks), o...  110 us
    pallas_call x1, Pallas kernels, on_device(): pl.pallas_call(functools.partial(outputs_kernel, 0.5 * people * n), grid=...  3.95 us

commit v1 on v0

v1 whole, which is shorter than its diff:
```python
import functools
import math

import jax
import jax.numpy as jnp
from jax import lax
from jax.experimental import pallas as pl
from jax.experimental.pallas import tpu as pltpu
from jax.sharding import PartitionSpec as P

LARGEST_TERM = 64.0

REDUCE_WIDE = (0, 5,)
GATHER_WIDE = (2,)
PLAN = {
    "P0": 12.910, "P1": 15.610, "P2": 15.620, "P3": 16.930, "P4": 17.370, "T0Y": 17.380, "T0Z": 17.380,
    "T1Z": 18.250, "T1Y": 18.310, "T2Y": 18.970, "T2Z": 19.380, "ARY": 19.770, "FIY": 19.780,
    "ARZ": 20.700, "FIZ": 21.680, "g1Z": 21.690, "OT": 21.690, "g1Y": 22.060, "g2Z": 22.700,
    "g3Z": 22.710, "h1Z": 22.750, "g2Y": 22.910, "h2Z": 23.400, "g3Y": 23.710, "LA": 25.800,
    "h3Z": 26.710, "U1": 26.720, "U2": 26.730,
}


def plan(length):
    if length == 4:
        return PLAN
    steps = {"P0": -3.0, "P1": -2.9, "P2": -2.8, "P3": -2.7, "P4": -2.6}
    for k in "YZ":
        for t in range(length - 1):
            steps[f"T{t}{k}"] = t + 0.9 - 0.02 * t
        steps["AR" + k] = length + 0.5
        steps["FI" + k] = length + 1.4
        for u in range(1, length):
            steps[f"g{u}{k}"] = length + 1 + u + 0.35 - 0.02 * u
            steps[f"h{u}Z"] = length + 2 + u + 0.34 - 0.02 * u
    steps["OT"] = length + 2.36
    steps["LA"] = 2 * length + 2.9
    steps["U1"] = 2 * length + 3.92
    steps["U2"] = 2 * length + 4.95
    return steps


def sweep_kernel(
    n, chunks, slots,
    geno_hbm, resid_ref, incl_hbm, mean_hbm, prior_ref, scale_ref,
    stat_out, eta,
    geno, incl, mean, core_out, core_in, pair_out, pair_in, own, line_out, line_in, eff,
    geno_sem, in_sem, core_ss, core_rs, pair_ss, pair_rs, line_ss, line_rs,
    gz_ss, gz_rs, gy_ss, gy_rs, gc_ss, gc_rs,
):
    length = n // 4
    owned = incl.shape[0]
    rows = owned // chunks
    people = resid_ref.shape[0]
    total = float(people * n)
    coding = 32760.0 / math.log(1.0 + LARGEST_TERM * total)
    me = lax.axis_index("ind")
    z = me // 4
    y = (me // 2) % 2
    c = me % 2

    def at(zz, yy, cc):
        return zz * 4 + yy * 2 + cc

    core_dev = {"ind": at(z, y, 1 - c)}
    pair_dev = {"ind": at(z, 1 - y, c)}
    up_dev = {"ind": at(lax.rem(z + 1, length), y, c)}
    down_dev = {"ind": at(lax.rem(z + length - 1, length), y, c)}
    has_up = z < length - 1
    has_down = z > 0

    def remote(src, dst, ss, rs, dev):
        return pltpu.make_async_remote_copy(
            src_ref=src, dst_ref=dst, send_sem=ss, recv_sem=rs,
            device_id=dev, device_id_type=pl.DeviceIdType.MESH,
        )

    def encode(x):
        code = (jnp.log(1.0 + jnp.abs(x)) * coding + 0.5).astype(jnp.int32)
        return jnp.where(x < 0.0, -code, code).astype(jnp.int16)

    def decode(code):
        level = code.astype(jnp.int32).astype(jnp.float32)
        size = jnp.exp(jnp.abs(level) * (1.0 / coding)) - 1.0
        return jnp.where(level < 0.0, -size, size)

    def loop(count, body):
        lax.fori_loop(0, count, lambda i, _: (body(i), 0)[1], 0)

    def for_z(body):
        loop(length, body)

    def place_of(zz, yy, cc):
        return (cc * 2 + yy) * length + zz

    def span(first, count=1):
        return pl.ds(pl.multiple_of(first * rows, math.gcd(rows, 128)), count * rows)

    def load(s, zz, yy, cc):
        q = place_of(zz, yy, cc)
        return pltpu.make_async_copy(
            geno_hbm.at[:, pl.ds(pl.multiple_of(at(zz, yy, cc) * owned + s * rows, 128), rows)],
            geno.at[s, :, span(q)], geno_sem.at[s, q],
        )

    owners = ((1 - y, 1 - c), (1 - y, c), (y, 1 - c), (y, c))

    def load_chunk(s):
        for yy, cc in owners:
            for_z(lambda i: load(s, i, yy, cc).start())

    loop(chunks, load_chunk)
    small = [
        pltpu.make_async_copy(incl_hbm, incl, in_sem.at[0]),
        pltpu.make_async_copy(mean_hbm, mean, in_sem.at[1]),
    ]
    for copy in small:
        copy.start()

    barrier = pltpu.get_barrier_semaphore()
    pl.semaphore_signal(barrier, inc=1, device_id=core_dev, device_id_type=pl.DeviceIdType.MESH)
    pl.semaphore_signal(barrier, inc=1, device_id=pair_dev, device_id_type=pl.DeviceIdType.MESH)

    @pl.when(has_up)
    def _():
        pl.semaphore_signal(barrier, inc=1, device_id=up_dev, device_id_type=pl.DeviceIdType.MESH)

    @pl.when(has_down)
    def _():
        pl.semaphore_signal(barrier, inc=1, device_id=down_dev, device_id_type=pl.DeviceIdType.MESH)

    pl.semaphore_wait(barrier, 2 + has_up.astype(jnp.int32) + has_down.astype(jnp.int32))

    for copy in small:
        copy.wait()
    eta[...] = jnp.zeros_like(eta)
    scale = scale_ref[...]
    shrink = scale / (1.0 + scale)
    bias = prior_ref[...] - 0.5 * jnp.log1p(scale)
    curve = 0.5 * total * shrink

    def among(s, which):
        found = s < 0
        for k in which:
            found = found | (s == k)
        return found

    def reduce_wide(s):
        return among(s, REDUCE_WIDE)

    def gather_wide(s):
        return among(s, GATHER_WIDE)

    def product(s, yy, cc, out):
        for_z(lambda i: load(s, i, yy, cc).wait())

        def piece(j):
            out[span(4 * j, 4), :] = lax.dot_general(
                geno[s, :, span(place_of(4 * j, yy, cc), 4)], resid_ref[...], (((0,), (0,)), ((), ())),
                preferred_element_type=jnp.float32,
            )

        loop(length // 4, piece)

    def core_copy(s, h):
        k = lax.rem(s, slots)
        return remote(
            core_out.at[k, h], core_in.at[s, h], core_ss.at[s, h], core_rs.at[s, h], core_dev
        )

    def pair_copy(s):
        return remote(pair_out.at[s], pair_in.at[s], pair_ss.at[s], pair_rs.at[s], pair_dev)

    def pair_last(s):
        return remote(
            pair_out.at[s, span(0)], pair_in.at[s, span(0)], pair_ss.at[s], pair_rs.at[s], pair_dev
        )

    def line_copy(s, t, d, g):
        return remote(
            line_out.at[s, t, d, g], line_in.at[s, t, d, g], line_ss.at[s, t, d, g], line_rs.at[s, t, d, g],
            up_dev if d == 0 else down_dev,
        )

    def to_core(s, h, yy):
        @pl.when(s >= slots)
        def _():
            core_copy(s - slots, h).wait_send()

        product(s, yy, 1 - c, core_out.at[lax.rem(s, slots), h])
        core_copy(s, h).start()

    def first_core(s):
        to_core(s, 0, 1 - y)

    def first_own(s):
        product(s, 1 - y, c, own.at[s, 1])

    def first_pair(s):
        core_copy(s, 0).wait_recv()

        @pl.when(jnp.logical_not(reduce_wide(s)))
        def _():
            def piece(j):
                part = span(4 * j, 4)
                pair_out[s, part] = encode(own[s, 1, part] + core_in[s, 0, part])

            loop(length // 4, piece)
            pair_copy(s).start()

        @pl.when(reduce_wide(s))
        def _():
            def piece(j):
                part = span(4 * j, 4)
                own[s, 1, part] = own[s, 1, part] + core_in[s, 0, part]

            loop(length // 4, piece)

    def second_core(s):
        to_core(s, 1, y)
        product(s, y, c, own.at[s, 0])

    def second_own(s):
        core_copy(s, 1).wait_recv()

        def piece(j):
            part = span(4 * j, 4)
            own[s, 0, part] = own[s, 0, part] + core_in[s, 1, part]

        loop(length // 4, piece)

    def along(s, t, wide):
        if t == 0 and not wide:
            pair_copy(s).wait_recv()

            def piece(j):
                part = span(4 * j, 4)
                own[s, 0, part] = own[s, 0, part] + decode(pair_in[s, part])

            loop(length // 4, piece)

        for d in range(2):
            place = z if d == 0 else length - 1 - z
            block = length - 1 - t + z if d == 0 else t - (length - 1 - z)

            for g in range(2 if wide else 1):
                @pl.when((place == 0) & (place < length - 1))
                def _():
                    line_out[s, t, d, g] = encode(own[s, g, span(block)])
                    line_copy(s, t, d, g).start()

                if t > 0:
                    @pl.when((place > 0) & (place <= t) & (place < length - 1))
                    def _():
                        line_copy(s, t - 1, d, g).wait_recv()
                        line_out[s, t, d, g] = encode(own[s, g, span(block)] + decode(line_in[s, t - 1, d, g]))
                        line_copy(s, t, d, g).start()

    def arrive(s, wide):
        for g in range(2 if wide else 1):
            for d in range(2):
                @pl.when(has_down if d == 0 else has_up)
                def _():
                    line_copy(s, length - 2, d, g).wait_recv()
                    own[s, g, span(z)] = own[s, g, span(z)] + decode(line_in[s, length - 2, d, g])

        if wide:
            pair_out[s, span(0)] = encode(own[s, 1, span(z)])
            pair_last(s).start()

    def gz_copy(s, u, d, f):
        k, q = 2 * s + f, span(place_of(z - u if d == 0 else z + u, y if f == 0 else 1 - y, c))
        return remote(
            eff.at[s, q], eff.at[s, q], gz_ss.at[k, u, d], gz_rs.at[k, u, d], up_dev if d == 0 else down_dev
        )

    def gz_landed(s, u, d, f):
        k, q = 2 * s + f, span(place_of(z - 1 - u if d == 0 else z + 1 + u, y if f == 0 else 1 - y, c))
        return remote(
            eff.at[s, q], eff.at[s, q], gz_ss.at[k, u, d], gz_rs.at[k, u, d], up_dev if d == 0 else down_dev
        )

    def gy_copy(s, i, yy):
        q = span(place_of(i, yy, c))
        return remote(eff.at[s, q], eff.at[s, q], gy_ss.at[s, i], gy_rs.at[s, i], pair_dev)

    def gc_copy(s, i, yy, cc):
        q = span(place_of(i, yy, cc))
        return remote(eff.at[s, q], eff.at[s, q], gc_ss.at[s, yy, i], gc_rs.at[s, yy, i], core_dev)

    def use(s, cc):
        def piece(j):
            q = span(place_of(0, 0, cc) + 8 * j, 8)
            eta[...] += jnp.dot(geno[s, :, q], eff[s, q], preferred_element_type=jnp.float32)

        loop(length // 4, piece)

    def send_own(s, f):
        @pl.when(has_up)
        def _():
            gz_copy(s, 0, 0, f).start()

        @pl.when(has_down)
        def _():
            gz_copy(s, 0, 1, f).start()

        gc_copy(s, z, y if f == 0 else 1 - y, c).start()

    def finish(s, wide):
        if wide:
            pair_last(s).wait_recv()
            own[s, 0, span(z)] = own[s, 0, span(z)] + decode(pair_in[s, span(0)])
        here = pl.ds(pl.multiple_of(s * rows, 8), rows)
        before = incl[here, :]
        stat = own[s, 0, span(z)] / total + before * mean[here, :]
        stat_out[here, :] = stat
        incl_new = 0.5 * before + 0.5 * jax.nn.sigmoid(bias + curve * stat * stat)
        eff[s, span(place_of(z, y, c))] = (incl_new * (stat * shrink)).astype(jnp.bfloat16)
        gy_copy(s, z, y).start()
        send_own(s, 0)

    def send_other(s):
        gy_copy(s, z, 1 - y).wait_recv()
        send_own(s, 1)

    def spread(s, u, f, wide):
        for d in range(2):
            source = z - u if d == 0 else z + u

            @pl.when((source >= 0) & (source < length))
            def _():
                gz_landed(s, u - 1, d, f).wait_recv()

                if u < length - 1:
                    @pl.when(has_up if d == 0 else has_down)
                    def _():
                        gz_copy(s, u, d, f).start()

                if not wide:
                    gy_copy(s, source, y).start()

                gc_copy(s, source, y if f == 0 else 1 - y, c).start()

    def from_pair(s):
        def take(i):
            gy_copy(s, i, 1 - y).wait_recv()
            gc_copy(s, i, 1 - y, c).start()

        for_z(take)

    def use_own(s):
        use(s, c)

    def use_core(s):
        def take(i):
            for yy in range(2):
                gc_copy(s, i, yy, 1 - c).wait_recv()

        for_z(take)
        use(s, 1 - c)

    tasks = {
        "P0": (None, None, first_core), "P1": (None, None, first_own), "P2": (None, None, first_pair),
        "P3": (None, None, second_core), "P4": (None, None, second_own),
        "OT": (gather_wide, True, send_other), "LA": (gather_wide, False, from_pair),
        "U1": (None, None, use_own), "U2": (None, None, use_core),
    }
    for kind in "YZ":
        wide = kind == "Z"
        for t in range(length - 1):
            tasks[f"T{t}{kind}"] = (reduce_wide, wide, functools.partial(along, t=t, wide=wide))
        tasks["AR" + kind] = (reduce_wide, wide, functools.partial(arrive, wide=wide))
        tasks["FI" + kind] = (reduce_wide, wide, functools.partial(finish, wide=wide))
        for u in range(1, length):
            tasks[f"g{u}{kind}"] = (gather_wide, wide, functools.partial(spread, u=u, f=0, wide=wide))
            if wide:
                tasks[f"h{u}Z"] = (gather_wide, True, functools.partial(spread, u=u, f=1, wide=True))

    steps = plan(length)
    least = min(math.floor(steps[name]) for name in tasks)
    late = {name: math.floor(steps[name]) - least for name in tasks}
    order = sorted(tasks, key=lambda name: steps[name] - math.floor(steps[name]))

    def wave(w):
        for name in order:
            test, wanted, body = tasks[name]
            s = w - late[name]
            go = (s >= 0) & (s < chunks)
            if test is not None:
                go = go & (test(s) if wanted else jnp.logical_not(test(s)))

            @pl.when(go)
            def _():
                body(s)

    loop(chunks + max(late.values()), wave)

    def drain(s):
        @pl.when(s >= chunks - slots)
        def _():
            for h in range(2):
                core_copy(s, h).wait_send()

        @pl.when(reduce_wide(s))
        def _():
            pair_last(s).wait_send()

        @pl.when(jnp.logical_not(reduce_wide(s)))
        def _():
            pair_copy(s).wait_send()

        gy_copy(s, z, y).wait_send()

        @pl.when(jnp.logical_not(gather_wide(s)))
        def _():
            def sent(i):
                @pl.when(i != z)
                def _():
                    gy_copy(s, i, y).wait_send()

            for_z(sent)

        def step(t):
            for d in range(2):
                place = z if d == 0 else length - 1 - z
                origin = z - t if d == 0 else z + t

                @pl.when((place <= t) & (place < length - 1))
                def _():
                    line_copy(s, t, d, 0).wait_send()

                    @pl.when(reduce_wide(s))
                    def _():
                        line_copy(s, t, d, 1).wait_send()

                @pl.when((origin >= 0) & (origin < length) & (place < length - 1))
                def _():
                    gz_copy(s, t, d, 0).wait_send()

                    @pl.when(gather_wide(s))
                    def _():
                        gz_copy(s, t, d, 1).wait_send()

        loop(length - 1, step)

        def blocks(i):
            for yy in range(2):
                gc_copy(s, i, yy, c).wait_send()

        for_z(blocks)

    loop(chunks, drain)


def outputs_kernel(
    half_total, stat_ref, incl_ref, eta_ref, labels_ref, prior_ref, scale_ref, offset_ref,
    incl_out, mean_out, resid_out,
):
    scale = scale_ref[...]
    shrink = scale / (1.0 + scale)
    bias = prior_ref[...] - 0.5 * jnp.log1p(scale)
    stat = stat_ref[...]
    mean_out[...] = stat * shrink
    logit = bias + (half_total * shrink) * stat * stat
    incl_out[...] = 0.5 * incl_ref[...] + 0.5 * jax.nn.sigmoid(logit)
    resid_out[...] = 4.0 * (
        labels_ref[...].astype(jnp.float32) - jax.nn.sigmoid(eta_ref[...] + offset_ref[...])
    )


def on_device(genotype, residual, labels, incl_old, mean_old, prior_logit, slab_scale, offset):
    n = lax.axis_size("ind")
    people, _ = genotype.shape
    owned, columns = incl_old.shape
    length = n // 4
    chunks = max(1, min(8, owned // 128))
    slots = max(1, min(chunks // 2, 3))
    rows = owned // chunks
    f32, bf16, i16 = jnp.float32, jnp.bfloat16, jnp.int16
    anywhere = pl.BlockSpec(memory_space=pl.ANY)
    vmem = pl.BlockSpec(memory_space=pltpu.VMEM)
    dma = pltpu.SemaphoreType.DMA
    hops = length - 1
    prior, scale, shift = (v.reshape(1, -1) for v in (prior_logit, slab_scale, offset))
    stat, eta = pl.pallas_call(
        functools.partial(sweep_kernel, n, chunks, slots),
        out_shape=(
            jax.ShapeDtypeStruct((owned, columns), f32),
            jax.ShapeDtypeStruct((people, columns), f32),
        ),
        in_specs=[anywhere, vmem, anywhere, anywhere, vmem, vmem],
        out_specs=(vmem, vmem),
        scratch_shapes=[
            pltpu.VMEM((chunks, people, n * rows), bf16),
            pltpu.VMEM(incl_old.shape, f32),
            pltpu.VMEM(mean_old.shape, f32),
            pltpu.VMEM((slots, 2, length * rows, columns), f32),
            pltpu.VMEM((chunks, 2, length * rows, columns), f32),
            pltpu.VMEM((chunks, length * rows, columns), i16),
            pltpu.VMEM((chunks, length * rows, columns), i16),
            pltpu.VMEM((chunks, 2, length * rows, columns), f32),
            pltpu.VMEM((chunks, hops, 2, 2, rows, columns), i16),
            pltpu.VMEM((chunks, hops, 2, 2, rows, columns), i16),
            pltpu.VMEM((chunks, n * rows, columns), bf16),
            dma((chunks, n)),
            dma((2,)),
            dma((chunks, 2)),
            dma((chunks, 2)),
            dma((chunks,)),
            dma((chunks,)),
            dma((chunks, hops, 2, 2)),
            dma((chunks, hops, 2, 2)),
            dma((2 * chunks, hops, 2)),
            dma((2 * chunks, hops, 2)),
            dma((chunks, length)),
            dma((chunks, length)),
            dma((chunks, 2, length)),
            dma((chunks, 2, length)),
        ],
        compiler_params=pltpu.CompilerParams(
            collective_id=0, has_side_effects=True, vmem_limit_bytes=67043328
        ),
        name="sweep",
    )(genotype, residual, incl_old, mean_old, prior, scale)

    steps = 4 if owned % 32 == 0 and people % 32 == 0 else 1
    upper = pl.BlockSpec((owned // steps, columns), lambda i: (i, 0))
    lower = pl.BlockSpec((people // steps, columns), lambda i: (i, 0))
    flat = pl.BlockSpec((1, columns), lambda i: (0, 0))
    return pl.pallas_call(
        functools.partial(outputs_kernel, 0.5 * people * n),
        grid=(steps,),
        out_shape=(
            jax.ShapeDtypeStruct((owned, columns), f32),
            jax.ShapeDtypeStruct((owned, columns), f32),
            jax.ShapeDtypeStruct((people, columns), f32),
        ),
        in_specs=[upper, upper, lower, lower, flat, flat, flat],
        out_specs=(upper, upper, lower),
        name="outputs",
    )(stat, incl_old, eta, labels, prior, scale, shift)


def solution(mesh):
    placed = (
        P(("groups", "ind"), None),
        P(("groups", "ind"), None),
        P(("groups", "ind"), None),
        P(("groups", "ind"), None),
        P(("groups", "ind"), None),
        P(),
        P(),
        P(),
    )
    return jax.shard_map(
        on_device,
        mesh=mesh,
        in_specs=placed,
        out_specs=(
            P(("groups", "ind"), None),
            P(("groups", "ind"), None),
            P(("groups", "ind"), None),
        ),
        check_vma=False,
    )
```

time: 115 us -> 111 us (0.965)
  Pallas kernels: 114 us -> 110 us
    pallas_call x1, Pallas kernels: 110 us -> 106 us  [on_device(): pl.pallas_call(functools.partial(sweep_kernel, n, chunks, slots), out_sha...]
where the time goes in v1:
time: 111 us
  Pallas kernels  110 us (99%)
    pallas_call x1, Pallas kernels, on_device(): pl.pallas_call(functools.partial(sweep_kernel, n, chunks, slots), out_sha...  106 us
    pallas_call x1, Pallas kernels, on_device(): pl.pallas_call(functools.partial(outputs_kernel, 0.5 * people * n), grid=...  3.95 us

profile of v1, /device:TPU:0, one launch (start us, length us, event | category | flops | bytes accessed | tf_op | source)
XLA Modules:
  0.0 110.6 jit_solution(8104659329121821980)
XLA Ops:
  0.6 106.0 %sweep.1 = (f32[1024,256]{1,0:T(8,128)}, f32[384,256]{1,0:T(8,128)}) custom-call(bf16[384,16384]{1,0:T(8,128)(2,1)} %geno_hbm.1, bf16[384,256]{1,0:T(8,128)(2,1)} %resid_ref.1, f32[1024,256]{1,0:T(8,128)} %incl_ref.1, f32[1024,256]{1,0:T(8,128)} %mean_hbm.1, f32[1,256]{1,0:T(1,128)} %bitcast.3, f32[1,256]{1,0:T(1,128)} %bitcast.5), custom_call_target="tpu_custom_call" | custom-call | tf_op jit(solution)/shard_map/sweep/pallas_call | solution.py:485
  106.6 4.0 %outputs.1 = (f32[1024,256]{1,0:T(8,128)}, f32[1024,256]{1,0:T(8,128)}, f32[384,256]{1,0:T(8,128)}) custom-call(f32[1024,256]{1,0:T(8,128)} %get-tuple-element.5.stat_ref, f32[1024,256]{1,0:T(8,128)} %incl_ref.1, f32[384,256]{1,0:T(8,128)} %get-tuple-element.6.eta_ref, s32[384,256]{1,0:T(8,128)} %labels_ref.1, f32[1,256]{1,0:T(1,128)} %bitcast.4, ...), custom_call_target="tpu_custom_call" | custom-call | tf_op jit(solution)/shard_map/outputs/pallas_call | solution.py:530

commit v2 on v1

v2 whole, which is shorter than its diff:
```python
import functools
import math

import jax
import jax.numpy as jnp
from jax import lax
from jax.experimental import pallas as pl
from jax.experimental.pallas import tpu as pltpu
from jax.sharding import PartitionSpec as P

LARGEST_TERM = 64.0

REDUCE_WIDE = (2, 6,)
GATHER_WIDE = (5,)
PLAN = {
    "P0": -10.032, "P1": -9.486, "P3": -9.133, "P2": -8.792, "P4": -8.681, "E0Z": -8.235, "E1Z": -7.941,
    "T1Z": -7.542, "D0Y": -7.169, "E0Y": -7.165, "E2Z": -6.876, "T2Z": -6.771, "D1Y": -6.701,
    "E1Y": -6.697, "T1Y": -6.070, "D2Y": -6.002, "ARZ": -5.824, "D3Y": -5.508, "E2Y": -5.073,
    "T2Y": -4.946, "ARY": -3.931, "FIZ": -3.901, "FIY": -3.855, "g1Y": -2.207, "g1Z": -2.031,
    "g2Y": -1.049, "OT": -0.847, "g3Y": -0.345, "h1Z": 1.041, "g2Z": 1.986, "g3Z": 3.677, "LA": 4.014,
    "h2Z": 4.121, "h3Z": 4.228, "U1": 4.766, "U2": 5.410,
}


def plan(length):
    if length == 4:
        return PLAN
    steps = {"P0": -3.0, "P1": -2.9, "P2": -2.8, "P3": -2.7, "P4": -2.6}
    for t in range(length):
        steps[f"D{t}Y"] = 0.5 + 0.01 * t
    for k in "YZ":
        for t in range(length - 1):
            steps[f"E{t}{k}"] = steps[f"T{t}{k}"] = t + 0.9 - 0.02 * t
        steps["AR" + k] = length + 0.5
        steps["FI" + k] = length + 1.4
        for u in range(1, length):
            steps[f"g{u}{k}"] = length + 1 + u + 0.35 - 0.02 * u
            steps[f"h{u}Z"] = length + 2 + u + 0.34 - 0.02 * u
    steps["OT"] = length + 2.36
    steps["LA"] = 2 * length + 2.9
    steps["U1"] = 2 * length + 4.92
    steps["U2"] = 2 * length + 5.95
    return steps


def sweep_kernel(
    n, chunks, per, slots,
    geno_hbm, resid_ref, incl_hbm, mean_hbm, prior_ref, scale_ref,
    stat_out, eta,
    geno, incl, mean, core_out, core_in, pair_out, pair_in, own, line_out, line_in, eff,
    geno_sem, in_sem, core_ss, core_rs, pair_ss, pair_rs, line_ss, line_rs,
    gz_ss, gz_rs, gy_ss, gy_rs, gc_ss, gc_rs,
):
    length = n // 4
    owned = incl.shape[0]
    rows = owned // chunks
    deep = per * rows
    people = resid_ref.shape[0]
    total = float(people * n)
    coding = 32760.0 / math.log(1.0 + LARGEST_TERM * total)
    me = lax.axis_index("ind")
    z = me // 4
    y = (me // 2) % 2
    c = me % 2

    def at(zz, yy, cc):
        return zz * 4 + yy * 2 + cc

    core_dev = {"ind": at(z, y, 1 - c)}
    pair_dev = {"ind": at(z, 1 - y, c)}
    up_dev = {"ind": at(lax.rem(z + 1, length), y, c)}
    down_dev = {"ind": at(lax.rem(z + length - 1, length), y, c)}
    has_up = z < length - 1
    has_down = z > 0

    def remote(src, dst, ss, rs, dev):
        return pltpu.make_async_remote_copy(
            src_ref=src, dst_ref=dst, send_sem=ss, recv_sem=rs,
            device_id=dev, device_id_type=pl.DeviceIdType.MESH,
        )

    def encode(x):
        code = (jnp.log(1.0 + jnp.abs(x)) * coding + 0.5).astype(jnp.int32)
        return jnp.where(x < 0.0, -code, code).astype(jnp.int16)

    def decode(code):
        level = code.astype(jnp.int32).astype(jnp.float32)
        size = jnp.exp(jnp.abs(level) * (1.0 / coding)) - 1.0
        return jnp.where(level < 0.0, -size, size)

    def loop(count, body):
        lax.fori_loop(0, count, lambda i, _: (body(i), 0)[1], 0)

    def for_z(body):
        loop(length, body)

    def place_of(zz, yy, cc):
        return (cc * 2 + yy) * length + zz

    def wide_span(first, count=1):
        return pl.ds(pl.multiple_of(first * deep, math.gcd(deep, 128)), count * deep)

    def span(s, q):
        return pl.ds(pl.multiple_of(q * deep + lax.rem(s, per) * rows, math.gcd(rows, 128)), rows)

    def nth(j):
        return pl.ds(pl.multiple_of(j * rows, math.gcd(rows, 128)), rows)

    def load(g, zz, yy, cc):
        q = place_of(zz, yy, cc)
        return pltpu.make_async_copy(
            geno_hbm.at[:, pl.ds(pl.multiple_of(at(zz, yy, cc) * owned + g * deep, 128), deep)],
            geno.at[g, :, wide_span(q)], geno_sem.at[g, q],
        )

    near = jnp.where(z < length - 1 - z, z, length - 1 - z)
    alone = length - 1 - 2 * near

    def far(j):
        k = j - alone
        side = jnp.where(k % 2 == 0, -1, 1)
        lone = jnp.where(z < length - 1 - z, length - 1 - j, j)
        return jnp.where(j < alone, lone, z + side * (near - k // 2))

    owners = ((1 - y, 1 - c), (1 - y, c), (y, 1 - c), (y, c))

    def load_group(g):
        for yy, cc in owners:
            for_z(lambda i: load(g, i, yy, cc).start())

    barrier = pltpu.get_barrier_semaphore()
    pl.semaphore_signal(barrier, inc=1, device_id=core_dev, device_id_type=pl.DeviceIdType.MESH)
    pl.semaphore_signal(barrier, inc=1, device_id=pair_dev, device_id_type=pl.DeviceIdType.MESH)

    @pl.when(has_up)
    def _():
        pl.semaphore_signal(barrier, inc=1, device_id=up_dev, device_id_type=pl.DeviceIdType.MESH)

    @pl.when(has_down)
    def _():
        pl.semaphore_signal(barrier, inc=1, device_id=down_dev, device_id_type=pl.DeviceIdType.MESH)

    small = [
        pltpu.make_async_copy(incl_hbm, incl, in_sem.at[0]),
        pltpu.make_async_copy(mean_hbm, mean, in_sem.at[1]),
    ]
    sets = chunks // per
    ahead = min(sets, 2)
    loop(ahead, load_group)
    for copy in small:
        copy.start()

    pl.semaphore_wait(barrier, 2 + has_up.astype(jnp.int32) + has_down.astype(jnp.int32))

    eta[...] = jnp.zeros_like(eta)
    scale = scale_ref[...]
    shrink = scale / (1.0 + scale)
    bias = prior_ref[...] - 0.5 * jnp.log1p(scale)
    curve = 0.5 * total * shrink

    def among(s, which):
        found = s < 0
        for k in which:
            found = found | (s == k)
        return found

    def reduce_wide(s):
        return among(s, REDUCE_WIDE)

    def gather_wide(s):
        return among(s, GATHER_WIDE)

    def product(g, yy, cc, out):
        for_z(lambda i: load(g, i, yy, cc).wait())

        def piece(j):
            out[wide_span(4 * j, 4), :] = lax.dot_general(
                geno[g, :, wide_span(place_of(4 * j, yy, cc), 4)], resid_ref[...], (((0,), (0,)), ((), ())),
                preferred_element_type=jnp.float32,
            )

        loop(length // 4, piece)

    def core_copy(g, h):
        return remote(
            core_out.at[lax.rem(g, slots), h], core_in.at[g, h], core_ss.at[g, h], core_rs.at[g, h], core_dev
        )

    def pair_copy(s, j):
        return remote(
            pair_out.at[s, nth(j)], pair_in.at[s, nth(j)], pair_ss.at[s], pair_rs.at[s, j], pair_dev
        )

    def pair_all(s):
        return remote(pair_out.at[s], pair_in.at[s], pair_ss.at[s], pair_rs.at[s, 0], pair_dev)

    def line_copy(s, t, d, f):
        return remote(
            line_out.at[s, t, d, f], line_in.at[s, t, d, f], line_ss.at[s, t, d, f], line_rs.at[s, t, d, f],
            up_dev if d == 0 else down_dev,
        )

    def to_core(g, h, yy):
        @pl.when(g >= slots)
        def _():
            core_copy(g - slots, h).wait_send()

        product(g, yy, 1 - c, core_out.at[lax.rem(g, slots), h])
        core_copy(g, h).start()

    def first_core(g):
        to_core(g, 0, 1 - y)

        @pl.when(g + ahead < sets)
        def _():
            load_group(g + ahead)

    def first_own(g):
        product(g, 1 - y, c, own.at[g, 1])

    def first_pair(g):
        core_copy(g, 0).wait_recv()

        def one(k):
            s = g * per + k

            @pl.when(jnp.logical_not(reduce_wide(s)))
            def _():
                def piece(j):
                    part = span(s, far(j))
                    pair_out[s, nth(j)] = encode(own[g, 1, part] + core_in[g, 0, part])
                    pair_copy(s, j).start()

                for_z(piece)

            @pl.when(reduce_wide(s))
            def _():
                def piece(j):
                    part = span(s, j)
                    own[g, 1, part] = own[g, 1, part] + core_in[g, 0, part]

                for_z(piece)

        loop(per, one)

    def second_core(g):
        to_core(g, 1, y)
        product(g, y, c, own.at[g, 0])

    def second_own(g):
        @pl.when(g == 0)
        def _():
            for copy in small:
                copy.wait()

        core_copy(g, 1).wait_recv()

        def piece(j):
            part = wide_span(4 * j, 4)
            own[g, 0, part] = own[g, 0, part] + core_in[g, 1, part]

        loop(length // 4, piece)

    def from_pair(s, j):
        part = span(s, far(j))
        pair_copy(s, j).wait_recv()
        own[s // per, 0, part] = own[s // per, 0, part] + decode(pair_in[s, nth(j)])

    def line_ends(s, t, wide):
        for d in range(2):
            place = z if d == 0 else length - 1 - z
            block = length - 1 - t if d == 0 else t

            @pl.when(place == 0)
            def _():
                for f in range(2 if wide else 1):
                    line_out[s, t, d, f] = encode(own[s // per, f, span(s, block)])
                    line_copy(s, t, d, f).start()

    def along(s, t, wide):
        for d in range(2):
            place = z if d == 0 else length - 1 - z
            block = length - 1 - t + z if d == 0 else t - (length - 1 - z)

            @pl.when((place > 0) & (place <= t) & (place < length - 1))
            def _():
                for f in range(2 if wide else 1):
                    line_copy(s, t - 1, d, f).wait_recv()
                    line_out[s, t, d, f] = encode(
                        own[s // per, f, span(s, block)] + decode(line_in[s, t - 1, d, f])
                    )
                    line_copy(s, t, d, f).start()

    def arrive(s, wide):
        mine = span(s, z)
        for f in range(2 if wide else 1):
            for d in range(2):
                @pl.when(has_down if d == 0 else has_up)
                def _():
                    line_copy(s, length - 2, d, f).wait_recv()
                    own[s // per, f, mine] = own[s // per, f, mine] + decode(line_in[s, length - 2, d, f])

        if wide:
            pair_out[s, nth(0)] = encode(own[s // per, 1, mine])
            pair_copy(s, 0).start()

    def gz_copy(s, u, d, f):
        k, q = 2 * s + f, span(s, place_of(z - u if d == 0 else z + u, y if f == 0 else 1 - y, c))
        return remote(
            eff.at[s // per, q], eff.at[s // per, q], gz_ss.at[k, u, d], gz_rs.at[k, u, d], up_dev if d == 0 else down_dev
        )

    def gz_landed(s, u, d, f):
        k, q = 2 * s + f, span(s, place_of(z - 1 - u if d == 0 else z + 1 + u, y if f == 0 else 1 - y, c))
        return remote(
            eff.at[s // per, q], eff.at[s // per, q], gz_ss.at[k, u, d], gz_rs.at[k, u, d], up_dev if d == 0 else down_dev
        )

    def gy_copy(s, i, yy):
        q = span(s, place_of(i, yy, c))
        return remote(eff.at[s // per, q], eff.at[s // per, q], gy_ss.at[s], gy_rs.at[s], pair_dev)

    def gc_copy(s, i, yy, cc):
        q = span(s, place_of(i, yy, cc))
        return remote(eff.at[s // per, q], eff.at[s // per, q], gc_ss.at[s], gc_rs.at[s], core_dev)

    def gy_all(s, yy):
        q = wide_span(place_of(0, yy, c), length)
        return remote(eff.at[s, q], eff.at[s, q], gy_ss.at[s], gy_rs.at[s], pair_dev)

    def gc_all(s, first, count):
        q = wide_span(first, count)
        return remote(eff.at[s, q], eff.at[s, q], gc_ss.at[s], gc_rs.at[s], core_dev)

    def use(g, cc):
        def piece(j):
            q = wide_span(place_of(0, 0, cc) + 8 * j, 8)
            eta[...] += jnp.dot(geno[g, :, q], eff[g, q], preferred_element_type=jnp.float32)

        loop(length // 4, piece)

    def send_own(s, f):
        @pl.when(has_up)
        def _():
            gz_copy(s, 0, 0, f).start()

        @pl.when(has_down)
        def _():
            gz_copy(s, 0, 1, f).start()

        gc_copy(s, z, y if f == 0 else 1 - y, c).start()

    def finish(s, wide):
        g, mine = s // per, span(s, z)
        if wide:
            pair_copy(s, 0).wait_recv()
            own[g, 0, mine] = own[g, 0, mine] + decode(pair_in[s, nth(0)])
        here = pl.ds(pl.multiple_of(s * rows, 8), rows)
        before = incl[here, :]
        stat = own[g, 0, mine] / total + before * mean[here, :]
        stat_out[here, :] = stat
        incl_new = 0.5 * before + 0.5 * jax.nn.sigmoid(bias + curve * stat * stat)
        eff[g, span(s, place_of(z, y, c))] = (incl_new * (stat * shrink)).astype(jnp.bfloat16)
        gy_copy(s, z, y).start()
        send_own(s, 0)

    def send_other(s):
        gy_copy(s, z, 1 - y).wait_recv()
        send_own(s, 1)

    def spread(s, u, f, wide):
        for d in range(2):
            source = z - u if d == 0 else z + u

            @pl.when((source >= 0) & (source < length))
            def _():
                gz_landed(s, u - 1, d, f).wait_recv()

                if u < length - 1:
                    @pl.when(has_up if d == 0 else has_down)
                    def _():
                        gz_copy(s, u, d, f).start()

                if not wide:
                    gy_copy(s, source, y).start()

                gc_copy(s, source, y if f == 0 else 1 - y, c).start()

    def last_pair(s):
        gy_all(s, 1 - y).wait_recv()
        gc_all(s, place_of(0, 1 - y, c), length).start()

    def drain(s):
        @pl.when((s % per == 0) & (s // per >= chunks // per - slots))
        def _():
            for h in range(2):
                core_copy(s // per, h).wait_send()

        @pl.when(reduce_wide(s))
        def _():
            pair_copy(s, 0).wait_send()

        @pl.when(jnp.logical_not(reduce_wide(s)))
        def _():
            pair_all(s).wait_send()

        @pl.when(gather_wide(s))
        def _():
            gy_copy(s, z, y).wait_send()

        @pl.when(jnp.logical_not(gather_wide(s)))
        def _():
            gy_all(s, y).wait_send()

        gc_all(s, place_of(0, 0, c), 2 * length).wait_send()

        def step(t):
            for d in range(2):
                place = z if d == 0 else length - 1 - z
                origin = z - t if d == 0 else z + t

                @pl.when((place <= t) & (place < length - 1))
                def _():
                    line_copy(s, t, d, 0).wait_send()

                    @pl.when(reduce_wide(s))
                    def _():
                        line_copy(s, t, d, 1).wait_send()

                @pl.when((origin >= 0) & (origin < length) & (place < length - 1))
                def _():
                    gz_copy(s, t, d, 0).wait_send()

                    @pl.when(gather_wide(s))
                    def _():
                        gz_copy(s, t, d, 1).wait_send()

        loop(length - 1, step)

    def use_own(g):
        use(g, c)

    def use_core(g):
        gc_all(g, place_of(0, 0, 1 - c), 2 * length).wait_recv()
        use(g, 1 - c)
        drain(g)

    groups = {
        "P0": first_core, "P1": first_own, "P2": first_pair, "P3": second_core, "P4": second_own,
        "U1": use_own, "U2": use_core,
    }
    tasks = {"OT": (gather_wide, True, send_other), "LA": (gather_wide, False, last_pair)}
    for j in range(length):
        tasks[f"D{j}Y"] = (reduce_wide, False, functools.partial(from_pair, j=j))
    for kind in "YZ":
        wide = kind == "Z"
        for t in range(length - 1):
            tasks[f"E{t}{kind}"] = (reduce_wide, wide, functools.partial(line_ends, t=t, wide=wide))
            if t > 0:
                tasks[f"T{t}{kind}"] = (reduce_wide, wide, functools.partial(along, t=t, wide=wide))
        tasks["AR" + kind] = (reduce_wide, wide, functools.partial(arrive, wide=wide))
        tasks["FI" + kind] = (reduce_wide, wide, functools.partial(finish, wide=wide))
        for u in range(1, length):
            tasks[f"g{u}{kind}"] = (gather_wide, wide, functools.partial(spread, u=u, f=0, wide=wide))
            if wide:
                tasks[f"h{u}Z"] = (gather_wide, True, functools.partial(spread, u=u, f=1, wide=True))

    steps = plan(length)
    names = [*groups, *tasks]
    least = min(math.floor(steps[name]) for name in names)
    late = {name: math.floor(steps[name]) - least for name in names}
    order = sorted(names, key=lambda name: steps[name] - math.floor(steps[name]))

    def wave(w):
        for name in order:
            s = w - late[name]
            go = (s >= 0) & (s < chunks)
            if name in groups:
                @pl.when(go & (s % per == 0))
                def _():
                    groups[name](s // per)
            else:
                test, wanted, body = tasks[name]

                @pl.when(go & (test(s) if wanted else jnp.logical_not(test(s))))
                def _():
                    body(s)

    loop(chunks + max(late.values()), wave)


def outputs_kernel(
    half_total, stat_ref, incl_ref, eta_ref, labels_ref, prior_ref, scale_ref, offset_ref,
    incl_out, mean_out, resid_out,
):
    scale = scale_ref[...]
    shrink = scale / (1.0 + scale)
    bias = prior_ref[...] - 0.5 * jnp.log1p(scale)
    stat = stat_ref[...]
    mean_out[...] = stat * shrink
    logit = bias + (half_total * shrink) * stat * stat
    incl_out[...] = 0.5 * incl_ref[...] + 0.5 * jax.nn.sigmoid(logit)
    resid_out[...] = 4.0 * (
        labels_ref[...].astype(jnp.float32) - jax.nn.sigmoid(eta_ref[...] + offset_ref[...])
    )


def on_device(genotype, residual, labels, incl_old, mean_old, prior_logit, slab_scale, offset):
    n = lax.axis_size("ind")
    people, _ = genotype.shape
    owned, columns = incl_old.shape
    length = n // 4
    per = 1
    chunks = per * max(1, min(8, owned // 128))
    sets = chunks // per
    slots = max(1, min(sets // 2, 3))
    rows = owned // chunks
    f32, bf16, i16 = jnp.float32, jnp.bfloat16, jnp.int16
    anywhere = pl.BlockSpec(memory_space=pl.ANY)
    vmem = pl.BlockSpec(memory_space=pltpu.VMEM)
    dma = pltpu.SemaphoreType.DMA
    hops = length - 1
    prior, scale, shift = (v.reshape(1, -1) for v in (prior_logit, slab_scale, offset))
    stat, eta = pl.pallas_call(
        functools.partial(sweep_kernel, n, chunks, per, slots),
        out_shape=(
            jax.ShapeDtypeStruct((owned, columns), f32),
            jax.ShapeDtypeStruct((people, columns), f32),
        ),
        in_specs=[anywhere, vmem, anywhere, anywhere, vmem, vmem],
        out_specs=(vmem, vmem),
        scratch_shapes=[
            pltpu.VMEM((sets, people, n * per * rows), bf16),
            pltpu.VMEM(incl_old.shape, f32),
            pltpu.VMEM(mean_old.shape, f32),
            pltpu.VMEM((slots, 2, length * per * rows, columns), f32),
            pltpu.VMEM((sets, 2, length * per * rows, columns), f32),
            pltpu.VMEM((chunks, length * rows, columns), i16),
            pltpu.VMEM((chunks, length * rows, columns), i16),
            pltpu.VMEM((sets, 2, length * per * rows, columns), f32),
            pltpu.VMEM((chunks, hops, 2, 2, rows, columns), i16),
            pltpu.VMEM((chunks, hops, 2, 2, rows, columns), i16),
            pltpu.VMEM((sets, n * per * rows, columns), bf16),
            dma((sets, n)),
            dma((2,)),
            dma((sets, 2)),
            dma((sets, 2)),
            dma((chunks,)),
            dma((chunks, length)),
            dma((chunks, hops, 2, 2)),
            dma((chunks, hops, 2, 2)),
            dma((2 * chunks, hops, 2)),
            dma((2 * chunks, hops, 2)),
            dma((chunks,)),
            dma((chunks,)),
            dma((chunks,)),
            dma((chunks,)),
        ],
        compiler_params=pltpu.CompilerParams(
            collective_id=0, has_side_effects=True, vmem_limit_bytes=67043328
        ),
        name="sweep",
    )(genotype, residual, incl_old, mean_old, prior, scale)

    steps = 2 if owned % 32 == 0 and people % 32 == 0 else 1
    upper = pl.BlockSpec((owned // steps, columns), lambda i: (i, 0))
    lower = pl.BlockSpec((people // steps, columns), lambda i: (i, 0))
    flat = pl.BlockSpec((1, columns), lambda i: (0, 0))
    return pl.pallas_call(
        functools.partial(outputs_kernel, 0.5 * people * n),
        grid=(steps,),
        out_shape=(
            jax.ShapeDtypeStruct((owned, columns), f32),
            jax.ShapeDtypeStruct((owned, columns), f32),
            jax.ShapeDtypeStruct((people, columns), f32),
        ),
        in_specs=[upper, upper, lower, lower, flat, flat, flat],
        out_specs=(upper, upper, lower),
        name="outputs",
    )(stat, incl_old, eta, labels, prior, scale, shift)


def solution(mesh):
    placed = (
        P(("groups", "ind"), None),
        P(("groups", "ind"), None),
        P(("groups", "ind"), None),
        P(("groups", "ind"), None),
        P(("groups", "ind"), None),
        P(),
        P(),
        P(),
    )
    return jax.shard_map(
        on_device,
        mesh=mesh,
        in_specs=placed,
        out_specs=(
            P(("groups", "ind"), None),
            P(("groups", "ind"), None),
            P(("groups", "ind"), None),
        ),
        check_vma=False,
    )
```

time: 111 us -> 101 us (0.910)
  Pallas kernels: 110 us -> 99.8 us
    pallas_call x1, Pallas kernels: 106 us -> 96.9 us  [on_device(): pl.pallas_call(functools.partial(sweep_kernel, n, chunks, per, slots), ou...]
where the time goes in v2:
time: 101 us; the launch traced here: 100 us
  Pallas kernels  99.8 us (99%)
    pallas_call x1, Pallas kernels, on_device(): pl.pallas_call(functools.partial(sweep_kernel, n, chunks, per, slots), ou...  96.9 us
    pallas_call x1, Pallas kernels, on_device(): pl.pallas_call(functools.partial(outputs_kernel, 0.5 * people * n), grid=...  2.92 us

profile of v2, /device:TPU:0, one launch (start us, length us, event | category | flops | bytes accessed | tf_op | source)
XLA Modules:
  0.0 100.4 jit_solution(3013543105424220839)
XLA Ops:
  0.6 96.9 %sweep.1 = (f32[1024,256]{1,0:T(8,128)}, f32[384,256]{1,0:T(8,128)}) custom-call(bf16[384,16384]{1,0:T(8,128)(2,1)} %geno_hbm.1, bf16[384,256]{1,0:T(8,128)(2,1)} %resid_ref.1, f32[1024,256]{1,0:T(8,128)} %incl_ref.1, f32[1024,256]{1,0:T(8,128)} %mean_hbm.1, f32[1,256]{1,0:T(1,128)} %bitcast.3, f32[1,256]{1,0:T(1,128)} %bitcast.5), custom_call_target="tpu_custom_call" | custom-call | tf_op jit(solution)/shard_map/sweep/pallas_call | solution.py:524
  97.5 2.9 %outputs.1 = (f32[1024,256]{1,0:T(8,128)}, f32[1024,256]{1,0:T(8,128)}, f32[384,256]{1,0:T(8,128)}) custom-call(f32[1024,256]{1,0:T(8,128)} %get-tuple-element.5.stat_ref, f32[1024,256]{1,0:T(8,128)} %incl_ref.1, f32[384,256]{1,0:T(8,128)} %get-tuple-element.6.eta_ref, s32[384,256]{1,0:T(8,128)} %labels_ref.1, f32[1,256]{1,0:T(1,128)} %bitcast.4, ...), custom_call_target="tpu_custom_call" | custom-call | tf_op jit(solution)/shard_map/outputs/pallas_call | solution.py:569

commit v3 on v2

--- a/solution.py
+++ b/solution.py
@@ -10,15 +10,15 @@
 
 LARGEST_TERM = 64.0
 
-REDUCE_WIDE = (2, 6,)
-GATHER_WIDE = (5,)
+REDUCE_WIDE = (0, 3, 7,)
+GATHER_WIDE = (2, 6, 7,)
 PLAN = {
-    "P0": -10.032, "P1": -9.486, "P3": -9.133, "P2": -8.792, "P4": -8.681, "E0Z": -8.235, "E1Z": -7.941,
-    "T1Z": -7.542, "D0Y": -7.169, "E0Y": -7.165, "E2Z": -6.876, "T2Z": -6.771, "D1Y": -6.701,
-    "E1Y": -6.697, "T1Y": -6.070, "D2Y": -6.002, "ARZ": -5.824, "D3Y": -5.508, "E2Y": -5.073,
-    "T2Y": -4.946, "ARY": -3.931, "FIZ": -3.901, "FIY": -3.855, "g1Y": -2.207, "g1Z": -2.031,
-    "g2Y": -1.049, "OT": -0.847, "g3Y": -0.345, "h1Z": 1.041, "g2Z": 1.986, "g3Z": 3.677, "LA": 4.014,
-    "h2Z": 4.121, "h3Z": 4.228, "U1": 4.766, "U2": 5.410,
+    "P0": 13.357, "P1": 13.631, "P3": 13.740, "P2": 14.320, "P4": 14.522, "E0Z": 14.526, "E1Z": 15.600,
+    "D0Y": 16.146, "D1Y": 16.150, "E0Y": 16.150, "T1Z": 16.216, "E2Z": 16.515, "E1Y": 17.469,
+    "T1Y": 17.615, "T2Z": 17.688, "D2Y": 17.728, "E2Y": 18.501, "ARZ": 18.788, "T2Y": 19.069,
+    "D3Y": 19.966, "ARY": 20.081, "FIY": 20.098, "FIZ": 20.170, "g1Z": 21.204, "g1Y": 21.855,
+    "g2Z": 22.258, "g2Y": 22.911, "OT": 23.318, "g3Z": 23.621, "g3Y": 24.145, "h1Z": 26.220,
+    "LAZ": 26.437, "LA": 26.522, "U1": 27.343, "U2": 27.730,
 }
 
 
@@ -35,9 +35,10 @@
         steps["FI" + k] = length + 1.4
         for u in range(1, length):
             steps[f"g{u}{k}"] = length + 1 + u + 0.35 - 0.02 * u
-            steps[f"h{u}Z"] = length + 2 + u + 0.34 - 0.02 * u
     steps["OT"] = length + 2.36
+    steps["h1Z"] = length + 3.34
     steps["LA"] = 2 * length + 2.9
+    steps["LAZ"] = 2 * length + 2.91
     steps["U1"] = 2 * length + 4.92
     steps["U2"] = 2 * length + 5.95
     return steps
@@ -71,6 +72,8 @@
     up_dev = {"ind": at(lax.rem(z + 1, length), y, c)}
     down_dev = {"ind": at(lax.rem(z + length - 1, length), y, c)}
     has_up = z < length - 1
+    even = z % 2 == 0
+    mate = z + 1 - 2 * (z % 2)
     has_down = z > 0
 
     def remote(src, dst, ss, rs, dev):
@@ -318,15 +321,15 @@
 
     def gy_copy(s, i, yy):
         q = span(s, place_of(i, yy, c))
-        return remote(eff.at[s // per, q], eff.at[s // per, q], gy_ss.at[s], gy_rs.at[s], pair_dev)
+        return remote(eff.at[s // per, q], eff.at[s // per, q], gy_ss.at[s], gy_rs.at[s, i], pair_dev)
 
     def gc_copy(s, i, yy, cc):
         q = span(s, place_of(i, yy, cc))
         return remote(eff.at[s // per, q], eff.at[s // per, q], gc_ss.at[s], gc_rs.at[s], core_dev)
 
-    def gy_all(s, yy):
-        q = wide_span(place_of(0, yy, c), length)
-        return remote(eff.at[s, q], eff.at[s, q], gy_ss.at[s], gy_rs.at[s], pair_dev)
+    def gy_sent(s, count):
+        q = wide_span(0, count)
+        return remote(eff.at[s, q], eff.at[s, q], gy_ss.at[s], gy_rs.at[s, 0], pair_dev)
 
     def gc_all(s, first, count):
         q = wide_span(first, count)
@@ -366,7 +369,27 @@
 
     def send_other(s):
         gy_copy(s, z, 1 - y).wait_recv()
-        send_own(s, 1)
+
+        @pl.when(even)
+        def _():
+            gz_copy(s, 0, 0, 1).start()
+
+        @pl.when(jnp.logical_not(even))
+        def _():
+            gz_copy(s, 0, 1, 1).start()
+
+        gc_copy(s, z, 1 - y, c).start()
+
+    def take_other(s):
+        @pl.when(even)
+        def _():
+            gz_landed(s, 0, 1, 1).wait_recv()
+
+        @pl.when(jnp.logical_not(even))
+        def _():
+            gz_landed(s, 0, 0, 1).wait_recv()
+
+        gc_copy(s, mate, 1 - y, c).start()
 
     def spread(s, u, f, wide):
         for d in range(2):
@@ -381,14 +404,27 @@
                     def _():
                         gz_copy(s, u, d, f).start()
 
-                if not wide:
+                if wide and u == 1:
+                    @pl.when(source != mate)
+                    def _():
+                        gy_copy(s, source, y).start()
+                else:
                     gy_copy(s, source, y).start()
 
                 gc_copy(s, source, y if f == 0 else 1 - y, c).start()
 
     def last_pair(s):
-        gy_all(s, 1 - y).wait_recv()
+        for_z(lambda i: gy_copy(s, i, 1 - y).wait_recv())
         gc_all(s, place_of(0, 1 - y, c), length).start()
+
+    def last_others(s):
+        def take(i):
+            @pl.when((i != z) & (i != mate))
+            def _():
+                gy_copy(s, i, 1 - y).wait_recv()
+                gc_copy(s, i, 1 - y, c).start()
+
+        for_z(take)
 
     def drain(s):
         @pl.when((s % per == 0) & (s // per >= chunks // per - slots))
@@ -406,11 +442,19 @@
 
         @pl.when(gather_wide(s))
         def _():
-            gy_copy(s, z, y).wait_send()
+            gy_sent(s, length - 1).wait_send()
+
+            @pl.when(even)
+            def _():
+                gz_copy(s, 0, 0, 1).wait_send()
+
+            @pl.when(jnp.logical_not(even))
+            def _():
+                gz_copy(s, 0, 1, 1).wait_send()
 
         @pl.when(jnp.logical_not(gather_wide(s)))
         def _():
-            gy_all(s, y).wait_send()
+            gy_sent(s, length).wait_send()
 
         gc_all(s, place_of(0, 0, c), 2 * length).wait_send()
 
@@ -431,10 +475,6 @@
                 def _():
                     gz_copy(s, t, d, 0).wait_send()
 
-                    @pl.when(gather_wide(s))
-                    def _():
-                        gz_copy(s, t, d, 1).wait_send()
-
         loop(length - 1, step)
 
     def use_own(g):
@@ -449,7 +489,10 @@
         "P0": first_core, "P1": first_own, "P2": first_pair, "P3": second_core, "P4": second_own,
         "U1": use_own, "U2": use_core,
     }
-    tasks = {"OT": (gather_wide, True, send_other), "LA": (gather_wide, False, last_pair)}
+    tasks = {
+        "OT": (gather_wide, True, send_other), "h1Z": (gather_wide, True, take_other),
+        "LA": (gather_wide, False, last_pair), "LAZ": (gather_wide, True, last_others),
+    }
     for j in range(length):
         tasks[f"D{j}Y"] = (reduce_wide, False, functools.partial(from_pair, j=j))
     for kind in "YZ":
@@ -462,8 +505,6 @@
         tasks["FI" + kind] = (reduce_wide, wide, functools.partial(finish, wide=wide))
         for u in range(1, length):
             tasks[f"g{u}{kind}"] = (gather_wide, wide, functools.partial(spread, u=u, f=0, wide=wide))
-            if wide:
-                tasks[f"h{u}Z"] = (gather_wide, True, functools.partial(spread, u=u, f=1, wide=True))
 
     steps = plan(length)
     names = [*groups, *tasks]
@@ -552,7 +593,7 @@
             dma((2 * chunks, hops, 2)),
             dma((2 * chunks, hops, 2)),
             dma((chunks,)),
-            dma((chunks,)),
+            dma((chunks, length)),
             dma((chunks,)),
             dma((chunks,)),
         ],

time: 101 us -> 97.8 us (0.968)
  Pallas kernels: 99.8 us -> 97 us
    pallas_call x1, Pallas kernels: 96.9 us -> 94.1 us  [on_device(): pl.pallas_call(functools.partial(sweep_kernel, n, chunks, per, slots), ou...]
where the time goes in v3:
time: 97.8 us; the launch traced here: 97.6 us
  Pallas kernels  97 us (99%)
    pallas_call x1, Pallas kernels, on_device(): pl.pallas_call(functools.partial(sweep_kernel, n, chunks, per, slots), ou...  94.1 us
    pallas_call x1, Pallas kernels, on_device(): pl.pallas_call(functools.partial(outputs_kernel, 0.5 * people * n), grid=...  2.92 us

profile of v3, /device:TPU:0, one launch (start us, length us, event | category | flops | bytes accessed | tf_op | source)
XLA Modules:
  0.0 97.6 jit_solution(16969980265984177579)
XLA Ops:
  0.6 94.1 %sweep.1 = (f32[1024,256]{1,0:T(8,128)}, f32[384,256]{1,0:T(8,128)}) custom-call(bf16[384,16384]{1,0:T(8,128)(2,1)} %geno_hbm.1, bf16[384,256]{1,0:T(8,128)(2,1)} %resid_ref.1, f32[1024,256]{1,0:T(8,128)} %incl_ref.1, f32[1024,256]{1,0:T(8,128)} %mean_hbm.1, f32[1,256]{1,0:T(1,128)} %bitcast.3, f32[1,256]{1,0:T(1,128)} %bitcast.5), custom_call_target="tpu_custom_call" | custom-call | tf_op jit(solution)/shard_map/sweep/pallas_call | solution.py:565
  94.7 2.9 %outputs.1 = (f32[1024,256]{1,0:T(8,128)}, f32[1024,256]{1,0:T(8,128)}, f32[384,256]{1,0:T(8,128)}) custom-call(f32[1024,256]{1,0:T(8,128)} %get-tuple-element.5.stat_ref, f32[1024,256]{1,0:T(8,128)} %incl_ref.1, f32[384,256]{1,0:T(8,128)} %get-tuple-element.6.eta_ref, s32[384,256]{1,0:T(8,128)} %labels_ref.1, f32[1,256]{1,0:T(1,128)} %bitcast.4, ...), custom_call_target="tpu_custom_call" | custom-call | tf_op jit(solution)/shard_map/outputs/pallas_call | solution.py:610

commit v4 on v3

--- a/solution.py
+++ b/solution.py
@@ -148,12 +148,12 @@
         pltpu.make_async_copy(mean_hbm, mean, in_sem.at[1]),
     ]
     sets = chunks // per
-    ahead = min(sets, 2)
+    ahead = 1
     loop(ahead, load_group)
+    pl.semaphore_wait(barrier, 2 + has_up.astype(jnp.int32) + has_down.astype(jnp.int32))
+
     for copy in small:
         copy.start()
-
-    pl.semaphore_wait(barrier, 2 + has_up.astype(jnp.int32) + has_down.astype(jnp.int32))
 
     eta[...] = jnp.zeros_like(eta)
     scale = scale_ref[...]

time: 97.8 us -> 97.8 us (level)
  no operation moved by 1% of the time
where the time goes in v4:
time: 97.8 us; the launch traced here: 97.6 us
  Pallas kernels  97 us (99%)
    pallas_call x1, Pallas kernels, on_device(): pl.pallas_call(functools.partial(sweep_kernel, n, chunks, per, slots), ou...  94.1 us
    pallas_call x1, Pallas kernels, on_device(): pl.pallas_call(functools.partial(outputs_kernel, 0.5 * people * n), grid=...  2.92 us

profile of v4, /device:TPU:0, one launch (start us, length us, event | category | flops | bytes accessed | tf_op | source)
XLA Modules:
  0.0 97.6 jit_solution(15027703888455025740)
XLA Ops:
  0.6 94.1 %sweep.1 = (f32[1024,256]{1,0:T(8,128)}, f32[384,256]{1,0:T(8,128)}) custom-call(bf16[384,16384]{1,0:T(8,128)(2,1)} %geno_hbm.1, bf16[384,256]{1,0:T(8,128)(2,1)} %resid_ref.1, f32[1024,256]{1,0:T(8,128)} %incl_ref.1, f32[1024,256]{1,0:T(8,128)} %mean_hbm.1, f32[1,256]{1,0:T(1,128)} %bitcast.3, f32[1,256]{1,0:T(1,128)} %bitcast.5), custom_call_target="tpu_custom_call" | custom-call | tf_op jit(solution)/shard_map/sweep/pallas_call | solution.py:565
  94.7 2.9 %outputs.1 = (f32[1024,256]{1,0:T(8,128)}, f32[1024,256]{1,0:T(8,128)}, f32[384,256]{1,0:T(8,128)}) custom-call(f32[1024,256]{1,0:T(8,128)} %get-tuple-element.5.stat_ref, f32[1024,256]{1,0:T(8,128)} %incl_ref.1, f32[384,256]{1,0:T(8,128)} %get-tuple-element.6.eta_ref, s32[384,256]{1,0:T(8,128)} %labels_ref.1, f32[1,256]{1,0:T(1,128)} %bitcast.4, ...), custom_call_target="tpu_custom_call" | custom-call | tf_op jit(solution)/shard_map/outputs/pallas_call | solution.py:610
